TPU v7x, 32 devices: a whole 2x2x4 slice. The times are simulated.
32 devices in a mesh: chan: 2 (over x), srow: 4 (over y, core), scol: 4 (over z).
Axes of the slice: x: 2, y: 2, z: 4, core: 2. Of those that a mesh axis runs over, the one named last changes fastest.
Arguments:
- vis: bfloat16 [2, 2, 512, 512], P('chan', None, 'srow', 'scol'), may hold values from -4 to 4
- model: bfloat16 [2, 64, 2, 512, 512], P('chan', None, None, 'srow', 'scol'), may hold values from -1 to 1, as said below
- flags: int32 [2, 32, 32], P('chan', 'srow', 'scol'), may hold values 0 or 1
- gains: float32 [2, 64, 2, 512], P('chan', None, None, ('srow', 'scol')), may hold values from -3 to 3
- consensus: float32 [64, 1, 2, 512], P(None, None, None, ('srow', 'scol')), may hold values from -3 to 3
- dual: float32 [2, 64, 2, 512], P('chan', None, None, ('srow', 'scol')), may hold values from -2 to 2
- rho: float32 [8], replicated, may hold values from 0.5 to 8
- cluster: int32 [64], replicated, may hold values from 0 to 7
Outputs:
- gains_out: float32 [2, 64, 2, 512], P('chan', None, None, ('srow', 'scol'))
- consensus_out: float32 [64, 1, 2, 512], P(None, None, None, ('srow', 'scol'))
- dual_out: float32 [2, 64, 2, 512], P('chan', None, None, ('srow', 'scol'))
Inputs may be any that keep to these rules, and one draw needn't show every extreme that they name: `model`: entries of about 1 / sqrt(512) in size.
All inputs are finite; a program needn't handle non-finite values. No bound on the sum of `flags` on one device may be relied on, other than what follows from the above.
Results may differ from a plain program's by a relative error of at most 0.0003.
Values sent between devices are 32-bit elements; how exact they have to be, the bound alone decides.
No kernel may reach another device: no remote copies, remote signals or barrier semaphores. Data moves between devices by JAX's collectives and lax.ppermute only.
A program may use at most 64 MiB of HBM per device.

v0:
```python
import math
import jax
import jax.numpy as jnp
from jax import lax
from jax.sharding import PartitionSpec as P

STATIONS = 512
TILE = 16
ITERS = 4
EPS = 1e-05
STEP = 0.5


def basis_table(groups, order):
    xval = (jnp.arange(groups, dtype=jnp.float32) + 0.5) / groups
    columns = [
        math.comb(order - 1, b) * xval**b * (1.0 - xval) ** (order - 1 - b) for b in range(order)
    ]
    return jnp.stack(columns, axis=1)


def local_terms(vis_block, model_block, weight, g_row, g_col):
    m_real = model_block[:, 0].astype(jnp.float32)
    m_imag = model_block[:, 1].astype(jnp.float32)
    c_real = g_col[:, 0][:, None, :]
    c_imag = g_col[:, 1][:, None, :]
    z_real = m_real * c_real + m_imag * c_imag
    z_imag = m_imag * c_real - m_real * c_imag
    r_real = g_row[:, 0][:, :, None]
    r_imag = g_row[:, 1][:, :, None]
    pred_real = jnp.sum(r_real * z_real - r_imag * z_imag, axis=0)
    pred_imag = jnp.sum(r_real * z_imag + r_imag * z_real, axis=0)
    res_real = vis_block[0].astype(jnp.float32) - pred_real
    res_imag = vis_block[1].astype(jnp.float32) - pred_imag
    w_real = weight * res_real
    w_imag = weight * res_imag
    power = jnp.sum(w_real * res_real + w_imag * res_imag)
    a_term = jnp.sum(weight[None] * (z_real * z_real + z_imag * z_imag), axis=-1)
    cross_real = jnp.sum(z_real * w_real[None] + z_imag * w_imag[None], axis=-1)
    cross_imag = jnp.sum(z_real * w_imag[None] - z_imag * w_real[None], axis=-1)
    return (power, a_term, jnp.stack([cross_real, cross_imag], axis=-2))


def solve(cross, a_term, g_now, target, rho_eff):
    denom = a_term + rho_eff[:, None]
    fresh = (cross + a_term[..., None, :] * g_now + rho_eff[:, None, None] * target) / denom[
        ..., None, :
    ]
    return g_now + STEP * (fresh - g_now)


def gram_solve(table, rhs):
    gram = jnp.dot(table.T, table, precision=lax.Precision.HIGHEST)
    factor = jnp.linalg.cholesky(gram)
    order = rhs.shape[1]
    flat = jnp.moveaxis(rhs, 1, 0).reshape(order, -1)
    sol = jax.scipy.linalg.cho_solve((factor, True), flat)
    return jnp.moveaxis(sol.reshape((order, rhs.shape[0]) + rhs.shape[2:]), 0, 1)


def sweep_terms(vis_block, model_block, weight, g_row, own_gains, rho_dir, groups):
    g_col = lax.all_gather(own_gains, "srow", axis=2, tiled=True)
    power, a_term, cross = local_terms(vis_block, model_block, weight, g_row, g_col)
    total = lax.psum(power, ("chan", "srow", "scol"))
    rho_eff = rho_dir * (total / (groups * STATIONS * STATIONS) + EPS)
    return (a_term, cross, rho_eff)


def shards(vis, model, flags, gains, consensus, dual, rho, cluster):
    groups = lax.axis_size("chan")
    order = consensus.shape[1]
    table = basis_table(groups, order)
    brow = lax.dynamic_index_in_dim(table, lax.axis_index("chan"), 0, keepdims=False)
    matches = cluster[:, None] == jnp.arange(rho.shape[0], dtype=jnp.int32)[None, :]
    rho_dir = jnp.sum(jnp.where(matches, rho[None, :], 0.0), axis=1)
    fl = flags[0].astype(jnp.float32)
    weight = jnp.repeat(jnp.repeat(fl, TILE, axis=0), TILE, axis=1)
    vis_block = vis[0]
    model_block = model[0]
    dual_own = dual[0]
    target = jnp.einsum("b,kbcp->kcp", brow, consensus, precision=lax.Precision.HIGHEST) - dual_own
    g = gains[0]
    for step in range(ITERS):
        g_row = lax.all_gather(g, "scol", axis=2, tiled=True)
        a_term, cross, rho_eff = sweep_terms(
            vis_block, model_block, weight, g_row, g, rho_dir, groups
        )
        a_own, cross_own = (
            lax.psum_scatter(a_term[:, None, :], "scol", scatter_dimension=2, tiled=True),
            lax.psum_scatter(cross, "scol", scatter_dimension=2, tiled=True),
        )
        g = solve(cross_own, a_own[:, 0, :], g, target, rho_eff)
    local = brow[None, :, None, None] * (g + dual_own)[:, None, :, :]
    sums = lax.psum(local, "chan")
    coeffs = gram_solve(table, sums)
    dual_new = (
        dual_own + g - jnp.einsum("b,kbcp->kcp", brow, coeffs, precision=lax.Precision.HIGHEST)
    )
    return (g[None], coeffs, dual_new[None])


def solution(mesh):
    placed = (
        P("chan", None, "srow", "scol"),
        P("chan", None, None, "srow", "scol"),
        P("chan", "srow", "scol"),
        P("chan", None, None, ("srow", "scol")),
        P(None, None, None, ("srow", "scol")),
        P("chan", None, None, ("srow", "scol")),
        P(),
        P(),
    )
    return jax.shard_map(
        shards,
        mesh=mesh,
        in_specs=placed,
        out_specs=(
            P("chan", None, None, ("srow", "scol")),
            P(None, None, None, ("srow", "scol")),
            P("chan", None, None, ("srow", "scol")),
        ),
        check_vma=False,
    )
```

profile of v0, /device:TPU:0, one launch (start us, length us, event | category | flops | bytes accessed | tf_op | source)
XLA Modules:
  0.0 436.5 jit_solution(12146551925661814514)
XLA Ops:
  7.2 15.3 %all-gather.1 = f32[1,64,2,128]{1,3,2,0:T(8,128)S(1)} all-gather(f32[1,64,2,32]{1,3,2,0:T(8,128)} %param.11), channel_id=3, replica_groups=mesh['chan'=2,'srow'=4,'scol'=4] {'scol'}, dimensions={3}, use_global_device_ids=true | all-gather | bytes 81920 | tf_op jit(solution)/shard_map/all_gather | solution.py:84
  22.5 5.6 %all-gather = f32[1,64,2,128]{1,3,2,0:T(8,128)S(1)} all-gather(f32[1,64,2,32]{1,3,2,0:T(8,128)} %param.11), channel_id=2, replica_groups=mesh['chan'=2,'srow'=4,'scol'=4] {'srow'}, dimensions={3}, use_global_device_ids=true | all-gather | bytes 81920 | tf_op jit(solution)/shard_map/all_gather | solution.py:62
  29.6 6.2 %subtract_reduce_fusion.7 = (f32[128,128]{1,0:T(8,128)S(1)}, f32[128,128]{1,0:T(8,128)S(1)}) fusion(f32[64,128]{1,0:T(8,128)S(1)} %copy.125, f32[64,128]{1,0:T(8,128)S(1)} %copy.124, f32[64,128]{1,0:T(8,128)S(1)} %copy.122, f32[64,128]{1,0:T(8,128)S(1)} %copy.121, bf16[64,2,128,128]{3,2,1,0:T(8,128)(2,1)} %bitcast.195), kind=kLoop, calls=%fused_computation.43 | loop fusion | flops 16744448 | bytes 4456448 | tf_op jit(solution)/shard_map/reduce_sum | solution.py:31
  36.4 4.1 add_reduce_fusion.6
  44.0 41.0 %psum.35 = f32[]{:T(128)} all-reduce(f32[]{:T(128)} %get-tuple-element.47), channel_id=1, replica_groups=mesh['chan'=2,'srow'=4,'scol'=4] {'chan','srow','scol'}, use_global_device_ids=true, to_apply=%region_9.10 | all-reduce | flops 1 | bytes 8 | tf_op jit(solution)/shard_map/psum | solution.py:64
  87.9 9.0 %all-reduce.9.cloned.1.call-done = f32[64,2,128]{0,1,2:T(2,128)} async-done(((f32[64,2,128]{0,1,2:T(2,128)}), f32[64,2,128]{0,1,2:T(2,128)}) %all-reduce.9.cloned.1.call-update) | async-done | bytes 65552
  97.8 13.5 %all_gather.27 = f32[64,2,128]{0,1,2:T(2,128)S(1)} all-gather(f32[64,2,32]{0,1,2:T(2,128)S(1)} %get-tuple-element.45), channel_id=1, replica_groups=mesh['chan'=2,'srow'=4,'scol'=4] {'scol'}, dimensions={2}, use_global_device_ids=true | all-gather | bytes 81920 | tf_op jit(solution)/shard_map/all_gather | solution.py:84
  111.3 5.4 %all_gather.26 = f32[64,2,128]{0,1,2:T(2,128)S(1)} all-gather(f32[64,2,32]{0,1,2:T(2,128)S(1)} %get-tuple-element.45), channel_id=1, replica_groups=mesh['chan'=2,'srow'=4,'scol'=4] {'srow'}, dimensions={2}, use_global_device_ids=true | all-gather | bytes 81920 | tf_op jit(solution)/shard_map/all_gather | solution.py:62
  117.3 6.2 %subtract_reduce_fusion.5 = (f32[128,128]{1,0:T(8,128)S(1)}, f32[128,128]{1,0:T(8,128)S(1)}) fusion(f32[64,128]{1,0:T(8,128)S(1)} %copy.136, f32[64,128]{1,0:T(8,128)S(1)} %copy.135, f32[64,128]{1,0:T(8,128)S(1)} %copy.134, f32[64,128]{1,0:T(8,128)S(1)} %copy.133, bf16[64,2,128,128]{3,2,1,0:T(8,128)(2,1)} %bitcast.196), kind=kLoop, calls=%fused_computation.38 | loop fusion | flops 16744448 | bytes 4456448 | tf_op jit(solution)/shard_map/reduce_sum | solution.py:31
  124.1 4.1 add_reduce_fusion.4
  129.0 39.0 %psum.36 = f32[]{:T(128)} all-reduce(f32[]{:T(128)} %get-tuple-element.42), channel_id=1, replica_groups=mesh['chan'=2,'srow'=4,'scol'=4] {'chan','srow','scol'}, use_global_device_ids=true, to_apply=%region_18.19 | all-reduce | flops 1 | bytes 8 | tf_op jit(solution)/shard_map/psum | solution.py:64
  170.3 33.9 %all-reduce.11.cloned.1.call-done = f32[64,2,128]{0,1,2:T(2,128)} async-done(((f32[64,2,128]{0,1,2:T(2,128)}), f32[64,2,128]{0,1,2:T(2,128)}) %all-reduce.11.cloned.1.call-update) | async-done | bytes 65552
  205.0 13.5 %all_gather.29 = f32[64,2,128]{0,1,2:T(2,128)S(1)} all-gather(f32[64,2,32]{0,1,2:T(2,128)S(1)} %multiply_add_fusion.2), channel_id=1, replica_groups=mesh['chan'=2,'srow'=4,'scol'=4] {'scol'}, dimensions={2}, use_global_device_ids=true | all-gather | bytes 81920 | tf_op jit(solution)/shard_map/all_gather | solution.py:84
  218.5 5.6 %all_gather.28 = f32[64,2,128]{0,1,2:T(2,128)S(1)} all-gather(f32[64,2,32]{0,1,2:T(2,128)S(1)} %multiply_add_fusion.2), channel_id=1, replica_groups=mesh['chan'=2,'srow'=4,'scol'=4] {'srow'}, dimensions={2}, use_global_device_ids=true | all-gather | bytes 81920 | tf_op jit(solution)/shard_map/all_gather | solution.py:62
  224.7 6.2 %subtract_reduce_fusion.3 = (f32[128,128]{1,0:T(8,128)S(1)}, f32[128,128]{1,0:T(8,128)S(1)}) fusion(f32[64,128]{1,0:T(8,128)S(1)} %copy.144, f32[64,128]{1,0:T(8,128)S(1)} %copy.143, f32[64,128]{1,0:T(8,128)S(1)} %copy.142, f32[64,128]{1,0:T(8,128)S(1)} %copy.141, bf16[64,2,128,128]{3,2,1,0:T(8,128)(2,1)} %bitcast.197), kind=kLoop, calls=%fused_computation.33 | loop fusion | flops 16744448 | bytes 4456448 | tf_op jit(solution)/shard_map/reduce_sum | solution.py:31
  236.4 38.9 %psum.37 = f32[]{:T(128)} all-reduce(f32[]{:T(128)} %get-tuple-element.39), channel_id=1, replica_groups=mesh['chan'=2,'srow'=4,'scol'=4] {'chan','srow','scol'}, use_global_device_ids=true, to_apply=%region_27.28 | all-reduce | flops 1 | bytes 8 | tf_op jit(solution)/shard_map/psum | solution.py:64
  277.6 33.9 %all-reduce.13.cloned.1.call-done = f32[64,2,128]{0,1,2:T(2,128)} async-done(((f32[64,2,128]{0,1,2:T(2,128)}), f32[64,2,128]{0,1,2:T(2,128)}) %all-reduce.13.cloned.1.call-update) | async-done | bytes 65552
  312.3 13.6 %all_gather.31 = f32[64,2,128]{0,1,2:T(2,128)S(1)} all-gather(f32[64,2,32]{0,1,2:T(2,128)S(1)} %multiply_add_fusion.1), channel_id=1, replica_groups=mesh['chan'=2,'srow'=4,'scol'=4] {'scol'}, dimensions={2}, use_global_device_ids=true | all-gather | bytes 81920 | tf_op jit(solution)/shard_map/all_gather | solution.py:84
  325.9 5.4 %all_gather.30 = f32[64,2,128]{0,1,2:T(2,128)S(1)} all-gather(f32[64,2,32]{0,1,2:T(2,128)S(1)} %multiply_add_fusion.1), channel_id=1, replica_groups=mesh['chan'=2,'srow'=4,'scol'=4] {'srow'}, dimensions={2}, use_global_device_ids=true | all-gather | bytes 81920 | tf_op jit(solution)/shard_map/all_gather | solution.py:62
  331.8 6.2 %subtract_reduce_fusion.1 = (f32[128,128]{1,0:T(8,128)S(1)}, f32[128,128]{1,0:T(8,128)S(1)}) fusion(f32[64,128]{1,0:T(8,128)S(1)} %copy.152, f32[64,128]{1,0:T(8,128)S(1)} %copy.151, f32[64,128]{1,0:T(8,128)S(1)} %copy.150, f32[64,128]{1,0:T(8,128)S(1)} %copy.149, bf16[64,2,128,128]{3,2,1,0:T(8,128)(2,1)} %bitcast.198), kind=kLoop, calls=%fused_computation.28 | loop fusion | flops 16744448 | bytes 4456448 | tf_op jit(solution)/shard_map/reduce_sum | solution.py:31
  338.6 4.1 add_reduce_fusion
  343.6 38.9 %psum.38 = f32[]{:T(128)} all-reduce(f32[]{:T(128)} %get-tuple-element.36), channel_id=1, replica_groups=mesh['chan'=2,'srow'=4,'scol'=4] {'chan','srow','scol'}, use_global_device_ids=true, to_apply=%region_36.37 | all-reduce | flops 1 | bytes 8 | tf_op jit(solution)/shard_map/psum | solution.py:64
  384.7 33.9 %all-reduce.15.cloned.1.call-done = f32[64,2,128]{0,1,2:T(2,128)} async-done(((f32[64,2,128]{0,1,2:T(2,128)}), f32[64,2,128]{0,1,2:T(2,128)}) %all-reduce.15.cloned.1.call-update) | async-done | bytes 65552
  420.1 8.3 %psum.39 = f32[64,1,2,32]{0,2,3,1:T(2,128)S(1)} all-reduce(f32[64,1,2,32]{0,2,3,1:T(2,128)S(1)} %get-tuple-element.34), channel_id=1, replica_groups=mesh['chan'=2,'srow'=4,'scol'=4] {'chan'}, use_global_device_ids=true, to_apply=%region_37.38 | all-reduce | flops 4096 | bytes 32768 | tf_op jit(solution)/shard_map/psum | solution.py:94
  (108 shorter events, 25.5 us)
Async XLA Ops:
  7.2 28.6 %copy-start.4 = (bf16[1,2,128,128]{3,2,1,0:T(8,128)(2,1)S(1)}, bf16[1,2,128,128]{3,2,1,0:T(8,128)(2,1)}, u32[]{:S(2)}) copy-start(bf16[1,2,128,128]{3,2,1,0:T(8,128)(2,1)} %param.8) | copy-start | bytes 196612
  7.2 80.0 %reduce-scatter.5.cloned.1.call-start = ((), (), s32[]{:S(2)}) async-start(), calls=%async_computation.4 | async-start | bytes 81920 | tf_op jit(solution)/shard_map/reduce_scatter | solution.py:89
  29.5 6.9 %copy-start = (bf16[1,64,2,128,128]{4,3,2,1,0:T(8,128)(2,1)S(1)}, bf16[1,64,2,128,128]{4,3,2,1,0:T(8,128)(2,1)}, u32[]{:S(2)}) copy-start(bf16[1,64,2,128,128]{4,3,2,1,0:T(8,128)(2,1)} %param.9) | copy-start | bytes 12582916
  29.5 13.3 %copy-start.10 = (u32[32]{0:T(128)S(1)}, u32[32]{0:T(128)}, u32[]{:S(2)}) copy-start(u32[32]{0:T(128)} %constant.53) | copy-start | bytes 388
  29.5 56.8 %copy-start.8 = (f32[8]{0:T(128)S(1)}, f32[8]{0:T(128)}, u32[]{:S(2)}) copy-start(f32[8]{0:T(128)} %param.14) | copy-start | bytes 100
  29.5 56.8 %copy-start.9 = (s32[64]{0:T(128)S(1)}, s32[64]{0:T(128)}, u32[]{:S(2)}) copy-start(s32[64]{0:T(128)} %param.15) | copy-start | bytes 772
  29.6 67.4 %copy-start.5 = (f32[1,64,2,32]{1,3,2,0:T(8,128)S(1)}, f32[1,64,2,32]{1,3,2,0:T(8,128)}, u32[]{:S(2)}) copy-start(f32[1,64,2,32]{1,3,2,0:T(8,128)} %param.11) | copy-start | bytes 49156
  29.6 67.4 %copy-start.6 = (f32[1,64,2,32]{1,3,2,0:T(8,128)S(1)}, f32[1,64,2,32]{1,3,2,0:T(8,128)}, u32[]{:S(2)}) copy-start(f32[1,64,2,32]{1,3,2,0:T(8,128)} %param.13) | copy-start | bytes 49156
  29.6 67.3 %copy-start.7 = (f32[64,1,2,32]{0,3,2,1:T(8,128)S(1)}, f32[64,1,2,32]{0,3,2,1:T(8,128)}, u32[]{:S(2)}) copy-start(f32[64,1,2,32]{0,3,2,1:T(8,128)} %param.12) | copy-start | bytes 49156
  41.3 55.6 %all-reduce.9.cloned.1.call-start = ((), (), s32[]{:S(2)}) async-start(), calls=%async_computation.8 | async-start | bytes 262144
  42.1 127.4 %reduce-scatter.7.cloned.1.call-start = ((), (), s32[]{:S(2)}) async-start(), calls=%async_computation.5 | async-start | bytes 81920 | tf_op jit(solution)/shard_map/reduce_scatter | solution.py:89
  117.3 6.8 %copy-start.1 = (bf16[1,64,2,128,128]{4,3,2,1,0:T(8,128)(2,1)S(1)}, bf16[1,64,2,128,128]{4,3,2,1,0:T(8,128)(2,1)}, u32[]{:S(2)}) copy-start(bf16[1,64,2,128,128]{4,3,2,1,0:T(8,128)(2,1)} %param.9) | copy-start | bytes 12582916
  129.0 75.2 %all-reduce.11.cloned.1.call-start = ((), (), s32[]{:S(2)}) async-start(), calls=%async_computation.9 | async-start | bytes 262144
  169.5 107.4 %reduce-scatter.9.cloned.1.call-start = ((), (), s32[]{:S(2)}) async-start(), calls=%async_computation.6 | async-start | bytes 81920 | tf_op jit(solution)/shard_map/reduce_scatter | solution.py:89
  224.6 6.8 %copy-start.2 = (bf16[1,64,2,128,128]{4,3,2,1,0:T(8,128)(2,1)S(1)}, bf16[1,64,2,128,128]{4,3,2,1,0:T(8,128)(2,1)}, u32[]{:S(2)}) copy-start(bf16[1,64,2,128,128]{4,3,2,1,0:T(8,128)(2,1)} %param.9) | copy-start | bytes 12582916
  236.4 75.1 %all-reduce.13.cloned.1.call-start = ((), (), s32[]{:S(2)}) async-start(), calls=%async_computation.10 | async-start | bytes 262144
  276.8 107.2 %reduce-scatter.11.cloned.1.call-start = ((), (), s32[]{:S(2)}) async-start(), calls=%async_computation.7 | async-start | bytes 81920 | tf_op jit(solution)/shard_map/reduce_scatter | solution.py:89
  331.8 6.8 %copy-start.3 = (bf16[1,64,2,128,128]{4,3,2,1,0:T(8,128)(2,1)S(1)}, bf16[1,64,2,128,128]{4,3,2,1,0:T(8,128)(2,1)}, u32[]{:S(2)}) copy-start(bf16[1,64,2,128,128]{4,3,2,1,0:T(8,128)(2,1)} %param.9) | copy-start | bytes 12582916
  343.5 75.1 %all-reduce.15.cloned.1.call-start = ((), (), s32[]{:S(2)}) async-start(), calls=%async_computation.11 | async-start | bytes 262144
Sparse Core Ops, SparseCore 0:
  41.4 20.3 reduce-scatter.4
  64.2 32.6 all-reduce.8
  129.1 18.5 reduce-scatter.6
  169.6 34.5 all-reduce.10
  236.5 18.5 reduce-scatter.8
  276.9 34.5 all-reduce.12
  343.6 18.5 reduce-scatter.10
  384.1 34.5 all-reduce.14
where the time goes:
time: 438 us; the launch traced here: 437 us
  blocking collectives  244 us (56%)
  waiting for transfers between devices  111 us (25%)
  other arithmetic  51.5 us (12%)
  between operations  19.1 us (4%)
  local copies, waits for them, and re-layouts  10.6 us (2%)
    psum x4, blocking collectives, sweep_terms(): total = lax.psum(power, ('chan', 'srow', 'scol'))  158 us
    unnamed x12, waiting for transfers between devices  111 us
    all_gather x4, blocking collectives, shards(): g_row = lax.all_gather(g, 'scol', axis=2, tiled=True)  55.9 us
    reduce_sum x4, other arithmetic, local_terms(): pred_real = jnp.sum(r_real * z_real - r_imag * z_imag, axis=0)  24.7 us
    all_gather x4, blocking collectives, sweep_terms(): g_col = lax.all_gather(own_gains, 'srow', axis=2, tiled=True)  22 us
    reduce_sum x4, other arithmetic, local_terms(): cross_real = jnp.sum(z_real * w_real[None] + z_imag * w_imag[None], axis=-1)  16.5 us
  transfers between devices with their start and end apart: 8, of which 4 were waited for; matrix products, arithmetic and copies ran while one was open for 2% of the time, Pallas kernels for 0%

commit v1 on v0

--- a/solution.py
+++ b/solution.py
@@ -61,7 +61,7 @@
 def sweep_terms(vis_block, model_block, weight, g_row, own_gains, rho_dir, groups):
     g_col = lax.all_gather(own_gains, "srow", axis=2, tiled=True)
     power, a_term, cross = local_terms(vis_block, model_block, weight, g_row, g_col)
-    total = lax.psum(power, ("chan", "srow", "scol"))
+    total = jnp.sum(lax.all_gather(power, axis_name=("chan", "srow", "scol")), 0)
     rho_eff = rho_dir * (total / (groups * STATIONS * STATIONS) + EPS)
     return (a_term, cross, rho_eff)
 

time: 438 us -> 441 us (level)
    psum x4 -> x0, blocking collectives: 158 us -> none  [sweep_terms(): total = lax.psum(power, ('chan', 'srow', 'scol'))]
    unnamed x0 -> x4, blocking collectives: none -> 157 us
where the time goes in v1:
time: 441 us; the launch traced here: 439 us
  blocking collectives  243 us (55%)
  waiting for transfers between devices  110 us (25%)
  other arithmetic  53.9 us (12%)
  between operations  19.2 us (4%)
  local copies, waits for them, and re-layouts  13.6 us (3%)
    unnamed x4, blocking collectives  157 us
    unnamed x12, waiting for transfers between devices  109 us
    all_gather x4, blocking collectives, shards(): g_row = lax.all_gather(g, 'scol', axis=2, tiled=True)  55.9 us
    reduce_sum x4, other arithmetic, local_terms(): pred_real = jnp.sum(r_real * z_real - r_imag * z_imag, axis=0)  24.7 us
    all_gather x4, blocking collectives, sweep_terms(): g_col = lax.all_gather(own_gains, 'srow', axis=2, tiled=True)  22 us
    reduce_sum x4, other arithmetic, local_terms(): cross_real = jnp.sum(z_real * w_real[None] + z_imag * w_imag[None], axis=-1)  16.5 us
  transfers between devices with their start and end apart: 8, of which 4 were waited for; matrix products, arithmetic and copies ran while one was open for 2% of the time, Pallas kernels for 0%

profile of v1, /device:TPU:0, one launch (start us, length us, event | category | flops | bytes accessed | tf_op | source)
XLA Modules:
  0.0 439.4 jit_solution(3203869359259579303)
XLA Ops:
  7.2 15.3 %all-gather.1 = f32[1,64,2,128]{1,3,2,0:T(8,128)S(1)} all-gather(f32[1,64,2,32]{1,3,2,0:T(8,128)} %param.11), channel_id=3, replica_groups=mesh['chan'=2,'srow'=4,'scol'=4] {'scol'}, dimensions={3}, use_global_device_ids=true | all-gather | bytes 81920 | tf_op jit(solution)/shard_map/all_gather | solution.py:84
  22.5 5.6 %all-gather = f32[1,64,2,128]{1,3,2,0:T(8,128)S(1)} all-gather(f32[1,64,2,32]{1,3,2,0:T(8,128)} %param.11), channel_id=2, replica_groups=mesh['chan'=2,'srow'=4,'scol'=4] {'srow'}, dimensions={3}, use_global_device_ids=true | all-gather | bytes 81920 | tf_op jit(solution)/shard_map/all_gather | solution.py:62
  29.6 6.2 %subtract_reduce_fusion.7 = (f32[128,128]{1,0:T(8,128)S(1)}, f32[128,128]{1,0:T(8,128)S(1)}) fusion(f32[64,128]{1,0:T(8,128)S(1)} %copy.125, f32[64,128]{1,0:T(8,128)S(1)} %copy.124, f32[64,128]{1,0:T(8,128)S(1)} %copy.122, f32[64,128]{1,0:T(8,128)S(1)} %copy.121, bf16[64,2,128,128]{3,2,1,0:T(8,128)(2,1)} %bitcast.199), kind=kLoop, calls=%fused_computation.43 | loop fusion | flops 16744448 | bytes 4456448 | tf_op jit(solution)/shard_map/reduce_sum | solution.py:31
  36.4 4.1 add_reduce_fusion.6
  44.8 40.5 %all-reduce = f32[32]{0:T(128)S(1)} all-reduce(f32[32]{0:T(128)S(1)} %dynamic-update-slice.3), channel_id=1, replica_groups=mesh['chan'=2,'srow'=4,'scol'=4] {'chan','srow','scol'}, use_global_device_ids=true, to_apply=%add | all-reduce | flops 32 | bytes 256
  88.8 8.1 %all-reduce.13.cloned.1.call-done = f32[64,2,128]{0,1,2:T(2,128)} async-done(((f32[64,2,128]{0,1,2:T(2,128)}), f32[64,2,128]{0,1,2:T(2,128)}) %all-reduce.13.cloned.1.call-update) | async-done | bytes 65552
  97.8 13.6 %all_gather.53 = f32[64,2,128]{0,1,2:T(2,128)S(1)} all-gather(f32[64,2,32]{0,1,2:T(2,128)S(1)} %get-tuple-element.45), channel_id=1, replica_groups=mesh['chan'=2,'srow'=4,'scol'=4] {'scol'}, dimensions={2}, use_global_device_ids=true | all-gather | bytes 81920 | tf_op jit(solution)/shard_map/all_gather | solution.py:84
  111.4 5.4 %all_gather.52 = f32[64,2,128]{0,1,2:T(2,128)S(1)} all-gather(f32[64,2,32]{0,1,2:T(2,128)S(1)} %get-tuple-element.45), channel_id=1, replica_groups=mesh['chan'=2,'srow'=4,'scol'=4] {'srow'}, dimensions={2}, use_global_device_ids=true | all-gather | bytes 81920 | tf_op jit(solution)/shard_map/all_gather | solution.py:62
  117.3 6.2 %subtract_reduce_fusion.5 = (f32[128,128]{1,0:T(8,128)S(1)}, f32[128,128]{1,0:T(8,128)S(1)}) fusion(f32[64,128]{1,0:T(8,128)S(1)} %copy.136, f32[64,128]{1,0:T(8,128)S(1)} %copy.135, f32[64,128]{1,0:T(8,128)S(1)} %copy.134, f32[64,128]{1,0:T(8,128)S(1)} %copy.133, bf16[64,2,128,128]{3,2,1,0:T(8,128)(2,1)} %bitcast.200), kind=kLoop, calls=%fused_computation.38 | loop fusion | flops 16744448 | bytes 4456448 | tf_op jit(solution)/shard_map/reduce_sum | solution.py:31
  124.2 4.1 add_reduce_fusion.4
  129.8 38.7 %all-reduce.1 = f32[32]{0:T(128)S(1)} all-reduce(f32[32]{0:T(128)S(1)} %dynamic-update-slice.4), channel_id=1, replica_groups=mesh['chan'=2,'srow'=4,'scol'=4] {'chan','srow','scol'}, use_global_device_ids=true, to_apply=%add.1 | all-reduce | flops 32 | bytes 256
  171.4 33.7 %all-reduce.15.cloned.1.call-done = f32[64,2,128]{0,1,2:T(2,128)} async-done(((f32[64,2,128]{0,1,2:T(2,128)}), f32[64,2,128]{0,1,2:T(2,128)}) %all-reduce.15.cloned.1.call-update) | async-done | bytes 65552
  205.9 13.5 %all_gather.57 = f32[64,2,128]{0,1,2:T(2,128)S(1)} all-gather(f32[64,2,32]{0,1,2:T(2,128)S(1)} %multiply_add_fusion.2), channel_id=1, replica_groups=mesh['chan'=2,'srow'=4,'scol'=4] {'scol'}, dimensions={2}, use_global_device_ids=true | all-gather | bytes 81920 | tf_op jit(solution)/shard_map/all_gather | solution.py:84
  219.5 5.6 %all_gather.56 = f32[64,2,128]{0,1,2:T(2,128)S(1)} all-gather(f32[64,2,32]{0,1,2:T(2,128)S(1)} %multiply_add_fusion.2), channel_id=1, replica_groups=mesh['chan'=2,'srow'=4,'scol'=4] {'srow'}, dimensions={2}, use_global_device_ids=true | all-gather | bytes 81920 | tf_op jit(solution)/shard_map/all_gather | solution.py:62
  225.6 6.2 %subtract_reduce_fusion.3 = (f32[128,128]{1,0:T(8,128)S(1)}, f32[128,128]{1,0:T(8,128)S(1)}) fusion(f32[64,128]{1,0:T(8,128)S(1)} %copy.144, f32[64,128]{1,0:T(8,128)S(1)} %copy.143, f32[64,128]{1,0:T(8,128)S(1)} %copy.142, f32[64,128]{1,0:T(8,128)S(1)} %copy.141, bf16[64,2,128,128]{3,2,1,0:T(8,128)(2,1)} %bitcast.201), kind=kLoop, calls=%fused_computation.33 | loop fusion | flops 16744448 | bytes 4456448 | tf_op jit(solution)/shard_map/reduce_sum | solution.py:31
  232.5 4.1 add_reduce_fusion.2
  238.1 38.7 %all-reduce.2 = f32[32]{0:T(128)S(1)} all-reduce(f32[32]{0:T(128)S(1)} %dynamic-update-slice.5), channel_id=1, replica_groups=mesh['chan'=2,'srow'=4,'scol'=4] {'chan','srow','scol'}, use_global_device_ids=true, to_apply=%add.2 | all-reduce | flops 32 | bytes 256
  279.7 33.7 %all-reduce.17.cloned.1.call-done = f32[64,2,128]{0,1,2:T(2,128)} async-done(((f32[64,2,128]{0,1,2:T(2,128)}), f32[64,2,128]{0,1,2:T(2,128)}) %all-reduce.17.cloned.1.call-update) | async-done | bytes 65552
  314.2 13.5 %all_gather.61 = f32[64,2,128]{0,1,2:T(2,128)S(1)} all-gather(f32[64,2,32]{0,1,2:T(2,128)S(1)} %multiply_add_fusion.1), channel_id=1, replica_groups=mesh['chan'=2,'srow'=4,'scol'=4] {'scol'}, dimensions={2}, use_global_device_ids=true | all-gather | bytes 81920 | tf_op jit(solution)/shard_map/all_gather | solution.py:84
  327.8 5.4 %all_gather.60 = f32[64,2,128]{0,1,2:T(2,128)S(1)} all-gather(f32[64,2,32]{0,1,2:T(2,128)S(1)} %multiply_add_fusion.1), channel_id=1, replica_groups=mesh['chan'=2,'srow'=4,'scol'=4] {'srow'}, dimensions={2}, use_global_device_ids=true | all-gather | bytes 81920 | tf_op jit(solution)/shard_map/all_gather | solution.py:62
  333.7 6.2 %subtract_reduce_fusion.1 = (f32[128,128]{1,0:T(8,128)S(1)}, f32[128,128]{1,0:T(8,128)S(1)}) fusion(f32[64,128]{1,0:T(8,128)S(1)} %copy.152, f32[64,128]{1,0:T(8,128)S(1)} %copy.151, f32[64,128]{1,0:T(8,128)S(1)} %copy.150, f32[64,128]{1,0:T(8,128)S(1)} %copy.149, bf16[64,2,128,128]{3,2,1,0:T(8,128)(2,1)} %bitcast.202), kind=kLoop, calls=%fused_computation.28 | loop fusion | flops 16744448 | bytes 4456448 | tf_op jit(solution)/shard_map/reduce_sum | solution.py:31
  346.2 38.7 %all-reduce.3 = f32[32]{0:T(128)S(1)} all-reduce(f32[32]{0:T(128)S(1)} %dynamic-update-slice.6), channel_id=1, replica_groups=mesh['chan'=2,'srow'=4,'scol'=4] {'chan','srow','scol'}, use_global_device_ids=true, to_apply=%add.3 | all-reduce | flops 32 | bytes 256
  387.8 33.8 %all-reduce.19.cloned.1.call-done = f32[64,2,128]{0,1,2:T(2,128)} async-done(((f32[64,2,128]{0,1,2:T(2,128)}), f32[64,2,128]{0,1,2:T(2,128)}) %all-reduce.19.cloned.1.call-update) | async-done | bytes 65552
  423.0 8.3 %psum.7 = f32[64,1,2,32]{0,2,3,1:T(2,128)S(1)} all-reduce(f32[64,1,2,32]{0,2,3,1:T(2,128)S(1)} %get-tuple-element.34), channel_id=1, replica_groups=mesh['chan'=2,'srow'=4,'scol'=4] {'chan'}, use_global_device_ids=true, to_apply=%region_37.38 | all-reduce | flops 4096 | bytes 32768 | tf_op jit(solution)/shard_map/psum | solution.py:94
  (120 shorter events, 30.9 us)
Async XLA Ops:
  7.2 28.6 %copy-start.4 = (bf16[1,2,128,128]{3,2,1,0:T(8,128)(2,1)S(1)}, bf16[1,2,128,128]{3,2,1,0:T(8,128)(2,1)}, u32[]{:S(2)}) copy-start(bf16[1,2,128,128]{3,2,1,0:T(8,128)(2,1)} %param.8) | copy-start | bytes 196612
  7.2 80.9 %reduce-scatter.5.cloned.1.call-start = ((), (), s32[]{:S(2)}) async-start(), calls=%async_computation.4 | async-start | bytes 81920 | tf_op jit(solution)/shard_map/reduce_scatter | solution.py:89
  29.5 6.9 %copy-start = (bf16[1,64,2,128,128]{4,3,2,1,0:T(8,128)(2,1)S(1)}, bf16[1,64,2,128,128]{4,3,2,1,0:T(8,128)(2,1)}, u32[]{:S(2)}) copy-start(bf16[1,64,2,128,128]{4,3,2,1,0:T(8,128)(2,1)} %param.9) | copy-start | bytes 12582916
  29.5 12.7 %copy-start.10 = (u32[32]{0:T(128)S(1)}, u32[32]{0:T(128)}, u32[]{:S(2)}) copy-start(u32[32]{0:T(128)} %constant.69) | copy-start | bytes 388
  29.5 57.2 %copy-start.8 = (f32[8]{0:T(128)S(1)}, f32[8]{0:T(128)}, u32[]{:S(2)}) copy-start(f32[8]{0:T(128)} %param.14) | copy-start | bytes 100
  29.5 57.2 %copy-start.9 = (s32[64]{0:T(128)S(1)}, s32[64]{0:T(128)}, u32[]{:S(2)}) copy-start(s32[64]{0:T(128)} %param.15) | copy-start | bytes 772
  29.6 67.4 %copy-start.5 = (f32[1,64,2,32]{1,3,2,0:T(8,128)S(1)}, f32[1,64,2,32]{1,3,2,0:T(8,128)}, u32[]{:S(2)}) copy-start(f32[1,64,2,32]{1,3,2,0:T(8,128)} %param.11) | copy-start | bytes 49156
  29.6 67.4 %copy-start.6 = (f32[1,64,2,32]{1,3,2,0:T(8,128)S(1)}, f32[1,64,2,32]{1,3,2,0:T(8,128)}, u32[]{:S(2)}) copy-start(f32[1,64,2,32]{1,3,2,0:T(8,128)} %param.13) | copy-start | bytes 49156
  29.6 67.4 %copy-start.7 = (f32[64,1,2,32]{0,3,2,1:T(8,128)S(1)}, f32[64,1,2,32]{0,3,2,1:T(8,128)}, u32[]{:S(2)}) copy-start(f32[64,1,2,32]{0,3,2,1:T(8,128)} %param.12) | copy-start | bytes 49156
  41.3 55.7 %all-reduce.13.cloned.1.call-start = ((), (), s32[]{:S(2)}) async-start(), calls=%async_computation.8 | async-start | bytes 262144
  42.1 128.5 %reduce-scatter.7.cloned.1.call-start = ((), (), s32[]{:S(2)}) async-start(), calls=%async_computation.5 | async-start | bytes 81920 | tf_op jit(solution)/shard_map/reduce_scatter | solution.py:89
  117.3 6.8 %copy-start.1 = (bf16[1,64,2,128,128]{4,3,2,1,0:T(8,128)(2,1)S(1)}, bf16[1,64,2,128,128]{4,3,2,1,0:T(8,128)(2,1)}, u32[]{:S(2)}) copy-start(bf16[1,64,2,128,128]{4,3,2,1,0:T(8,128)(2,1)} %param.9) | copy-start | bytes 12582916
  129.8 75.3 %all-reduce.15.cloned.1.call-start = ((), (), s32[]{:S(2)}) async-start(), calls=%async_computation.9 | async-start | bytes 262144
  170.6 108.4 %reduce-scatter.9.cloned.1.call-start = ((), (), s32[]{:S(2)}) async-start(), calls=%async_computation.6 | async-start | bytes 81920 | tf_op jit(solution)/shard_map/reduce_scatter | solution.py:89
  225.6 6.8 %copy-start.2 = (bf16[1,64,2,128,128]{4,3,2,1,0:T(8,128)(2,1)S(1)}, bf16[1,64,2,128,128]{4,3,2,1,0:T(8,128)(2,1)}, u32[]{:S(2)}) copy-start(bf16[1,64,2,128,128]{4,3,2,1,0:T(8,128)(2,1)} %param.9) | copy-start | bytes 12582916
  238.1 75.3 %all-reduce.17.cloned.1.call-start = ((), (), s32[]{:S(2)}) async-start(), calls=%async_computation.10 | async-start | bytes 262144
  278.9 108.1 %reduce-scatter.11.cloned.1.call-start = ((), (), s32[]{:S(2)}) async-start(), calls=%async_computation.7 | async-start | bytes 81920 | tf_op jit(solution)/shard_map/reduce_scatter | solution.py:89
  333.7 6.8 %copy-start.3 = (bf16[1,64,2,128,128]{4,3,2,1,0:T(8,128)(2,1)S(1)}, bf16[1,64,2,128,128]{4,3,2,1,0:T(8,128)(2,1)}, u32[]{:S(2)}) copy-start(bf16[1,64,2,128,128]{4,3,2,1,0:T(8,128)(2,1)} %param.9) | copy-start | bytes 12582916
  346.2 75.3 %all-reduce.19.cloned.1.call-start = ((), (), s32[]{:S(2)}) async-start(), calls=%async_computation.11 | async-start | bytes 262144
Sparse Core Ops, SparseCore 0:
  41.4 20.3 reduce-scatter.4
  64.2 32.6 all-reduce.12
  129.9 18.5 reduce-scatter.6
  170.7 34.3 all-reduce.14
  238.2 18.5 reduce-scatter.8
  279.0 34.3 all-reduce.16
  346.3 18.5 reduce-scatter.10
  387.1 34.3 all-reduce.18
